TPU v7x, 32 devices: a whole 2x2x4 slice. The times are simulated.
32 devices in a mesh: res: 8 (over z, y), ch: 4 (over x, core).
Axes of the slice: x: 2, y: 2, z: 4, core: 2. Of those that a mesh axis runs over, the one named last changes fastest.
Arguments:
- sequence_matrix: bfloat16 [8, 512, 256], P(None, 'res'), may hold values from -6 to 6
- couple_matrix: bfloat16 [32, 128, 4096], P('res', 'ch')
- block_target_entry: int32 [8, 4], P('res'), may hold values from 0 to 7, as said below
- block_present_flag: int32 [8, 4], P('res'), may hold values from 0 to 1, as said below
- amino_strand: int32 [512], P('res'), may hold values from 0 to 5, never falling along the last dimension, each value on 1 to 170 neighbouring positions
- sequence_scaling_factor: float32 [256], replicated, may hold values from 0.5 to 1.5
- query_key_value_matrix: bfloat16 [4, 256, 256], P(None, None, 'ch'), may hold values from -0.375 to 0.375
- focus_result_matrix: bfloat16 [256, 256], P('ch'), may hold values from -0.375 to 0.375
- strand_focus_offset: float32 [8], replicated, may hold values from -2 to 2
- couple_scaling_factor: float32 [128], P('ch'), may hold values from 0.5 to 1.5
- focus_offset_matrix: float32 [128, 8], P('ch')
- product_scaling_factor: float32 [256], replicated, may hold values from 0.5 to 1.5
- first_factor_matrix: bfloat16 [256, 32], replicated, may hold values from -0.375 to 0.375
- second_factor_matrix: bfloat16 [256, 32], P(None, 'ch'), may hold values from -0.375 to 0.375
- product_result_matrix: bfloat16 [128, 32, 32], P(None, None, 'ch'), may hold values from -0.8984375 to 0.8984375
- product_result_offset: float32 [128], P('ch'), may hold values from -3 to 3
Outputs:
- sequence_result_matrix: bfloat16 [8, 512, 256], P(None, 'res')
- pairwise_output: bfloat16 [32, 128, 4096], P('res', 'ch')
Inputs may be any that keep to these rules, and one draw needn't show every extreme that they name: `block_target_entry`: slot 0 of row tile r names r itself; the column tiles of one row tile are distinct. `block_present_flag`: the valid slots of each row tile are its first ones, two or more of them; in every draw some row tile has all 4 slots valid.
All inputs are finite; a program needn't handle non-finite values.
Results may differ from a plain program's by a relative error of at most 0.005.
Values may be sent and summed in bfloat16 or wider, within the bound.
No kernel may reach another device: no remote copies, remote signals or barrier semaphores. Data moves between devices by JAX's collectives and lax.ppermute only.
A program may use at most 128 MiB of HBM per device.

v0:
```python
import math
import jax
import jax.numpy as jnp
from jax import lax
from jax.sharding import PartitionSpec as P

C_Z = 128
FOCUS_NUMBER = 8
FOCUS_BREADTH = 32
PRODUCT_FEATURE = 32
EPS = 1e-05
MASKED = -1e30


def final_dimension_standardize(values, gain_vector):
    values = values.astype(jnp.float32)
    average = jnp.mean(values, axis=-1, keepdims=True)
    variance = jnp.mean(jnp.square(values - average), axis=-1, keepdims=True)
    return (values - average) * lax.rsqrt(variance + EPS) * gain_vector


def on_device(
    sequence_matrix,
    couple_matrix,
    block_target_entry,
    block_present_flag,
    amino_strand,
    sequence_scaling_factor,
    query_key_value_matrix,
    focus_result_matrix,
    strand_focus_offset,
    couple_scaling_factor,
    focus_offset_matrix,
    product_scaling_factor,
    first_factor_matrix,
    second_factor_matrix,
    product_result_matrix,
    product_result_offset,
):
    groups = lax.axis_size("ch")
    group_index = lax.axis_index("ch")
    local_heads = FOCUS_NUMBER // groups
    slot_count = couple_matrix.shape[0]
    cell_count = couple_matrix.shape[2]
    block_extent = sequence_matrix.shape[1]
    sequence_number_overall = sequence_matrix.shape[0]
    pair_field = couple_matrix.astype(jnp.float32)
    part_one = jnp.sum(pair_field, axis=1)
    part_two = jnp.sum(pair_field * pair_field, axis=1)
    sum_one, sum_two = lax.psum((part_one, part_two), "ch")
    center = sum_one / C_Z
    spread = lax.rsqrt(sum_two / C_Z - center * center + EPS)
    normed = (
        (pair_field - center[:, None, :])
        * spread[:, None, :]
        * couple_scaling_factor[None, :, None]
    )
    partial_value = jnp.einsum(
        "kcp,ch->hkp", normed, focus_offset_matrix, precision=lax.Precision.HIGHEST
    )
    head_bias = lax.psum_scatter(partial_value, "ch", scatter_dimension=0, tiled=True)
    head_bias = head_bias.astype(jnp.bfloat16)
    bias_all, cols_all, valid_all, chain_all = (
        lax.all_gather(head_bias, "res", axis=1, tiled=True),
        lax.all_gather(block_target_entry, "res", axis=0, tiled=True),
        lax.all_gather(block_present_flag, "res", axis=0, tiled=True),
        lax.all_gather(amino_strand, "res", axis=0, tiled=True),
    )
    sequence_first_layout = lax.all_to_all(
        sequence_matrix, "res", split_axis=0, concat_axis=1, tiled=True
    )
    device_rows, amino_number_here, sequence_feature_breadth = sequence_first_layout.shape
    tile_count = amino_number_here // block_extent
    sequence_standardized = final_dimension_standardize(
        sequence_first_layout, sequence_scaling_factor
    ).astype(jnp.bfloat16)
    projected_rows = jnp.einsum(
        "hbx,sxt->shbt",
        sequence_standardized,
        query_key_value_matrix,
        preferred_element_type=jnp.float32,
    ).astype(jnp.bfloat16)
    projected_rows = projected_rows.reshape(
        4, device_rows, tile_count, block_extent, local_heads, FOCUS_BREADTH
    )
    queries = projected_rows[0]
    keyset = projected_rows[1]
    valueset = projected_rows[2]
    gateset = projected_rows[3]
    chain_tiles = chain_all.reshape(tile_count, block_extent)
    bias_tiles = bias_all.reshape(local_heads, tile_count, slot_count, block_extent, block_extent)
    head_scale = lax.dynamic_slice_in_dim(
        strand_focus_offset, group_index * local_heads, local_heads, 0
    )
    block_tiles = math.gcd(tile_count, max(1, 512 // block_extent))

    def attend(block_index):
        first_tile = block_index * block_tiles
        columns = lax.dynamic_slice_in_dim(cols_all, first_tile, block_tiles, 0)
        usable = lax.dynamic_slice_in_dim(valid_all, first_tile, block_tiles, 0) > 0
        query_block = lax.dynamic_slice_in_dim(queries, first_tile, block_tiles, 1)
        key_block = keyset[:, columns]
        value_block = valueset[:, columns]
        scores = jnp.einsum(
            "rgahd,rgkbhd->rghakb", query_block, key_block, preferred_element_type=jnp.float32
        ) * FOCUS_BREADTH ** (-0.5)
        pair_part = lax.dynamic_slice_in_dim(bias_tiles, first_tile, block_tiles, 1).astype(
            jnp.float32
        )
        pair_part = pair_part.transpose(1, 0, 3, 2, 4)
        query_chain = lax.dynamic_slice_in_dim(chain_tiles, first_tile, block_tiles, 0)
        same_chain = (query_chain[:, :, None, None] == chain_tiles[columns][:, None, :, :]).astype(
            jnp.float32
        )
        scores = (
            scores
            + pair_part[None]
            + head_scale[None, None, :, None, None, None] * same_chain[None, :, None]
        )
        scores = jnp.where(usable[None, :, None, None, :, None], scores, MASKED)
        row_max = jnp.max(scores, axis=(4, 5), keepdims=True)
        exponent = jnp.exp(scores - row_max)
        attn_weights = (exponent / jnp.sum(exponent, axis=(4, 5), keepdims=True)).astype(
            jnp.bfloat16
        )
        mixed = jnp.einsum(
            "rghakb,rgkbhd->rgahd", attn_weights, value_block, preferred_element_type=jnp.float32
        )
        gate_block = lax.dynamic_slice_in_dim(gateset, first_tile, block_tiles, 1).astype(
            jnp.float32
        )
        return (mixed * jax.nn.sigmoid(gate_block)).astype(jnp.bfloat16)

    blocks = lax.map(attend, jnp.arange(tile_count // block_tiles, dtype=jnp.int32))
    attended_rows = blocks.transpose(1, 0, 2, 3, 4, 5).reshape(
        device_rows * amino_number_here, local_heads * FOCUS_BREADTH
    )
    residual_input = sequence_first_layout.reshape(
        device_rows * amino_number_here, sequence_feature_breadth
    )
    partial_out = jnp.dot(attended_rows, focus_result_matrix, preferred_element_type=jnp.float32)
    head_total = lax.psum(partial_out, "ch")
    updated_state = (
        (residual_input.astype(jnp.float32) + head_total)
        .astype(jnp.bfloat16)
        .reshape(device_rows, amino_number_here, sequence_feature_breadth)
    )
    sequence_result_matrix = lax.all_to_all(
        updated_state, "res", split_axis=1, concat_axis=0, tiled=True
    )
    outer_normed = (
        final_dimension_standardize(sequence_result_matrix, product_scaling_factor)
        .astype(jnp.bfloat16)
        .reshape(sequence_number_overall * block_extent, sequence_feature_breadth)
    )
    left_projected = (
        jnp.dot(outer_normed, first_factor_matrix, preferred_element_type=jnp.float32)
        .astype(jnp.bfloat16)
        .reshape(sequence_number_overall, block_extent * PRODUCT_FEATURE)
    )
    own_columns = block_target_entry[0]
    right_projected = (
        jnp.dot(outer_normed, second_factor_matrix, preferred_element_type=jnp.float32)
        .astype(jnp.bfloat16)
        .reshape(sequence_number_overall, block_extent, -1)
    )
    narrow = right_projected.shape[2]
    weight_flat = product_result_matrix.reshape(C_Z, PRODUCT_FEATURE * narrow)
    empty_tiles = jnp.zeros(
        (slot_count, sequence_number_overall, block_extent, narrow), jnp.bfloat16
    )
    shard_piece = lax.all_gather(right_projected, "res", axis=1, tiled=True)
    piece_rows = shard_piece.shape[1]
    offset = own_columns * block_extent
    inside = (offset >= 0) & (offset < piece_rows)

    def take_one(offset_one, inside_one, held_tile):
        taken = lax.dynamic_slice_in_dim(
            shard_piece, jnp.clip(offset_one, 0, piece_rows - block_extent), block_extent, 1
        )
        return jnp.where(inside_one, taken, held_tile)

    chosen = jax.vmap(take_one, in_axes=(0, 0, 0))(offset, inside, empty_tiles)
    left_turned = left_projected.T

    def outer_one(right_tile_rows):
        product = (
            jnp.dot(
                left_turned,
                right_tile_rows.reshape(sequence_number_overall, block_extent * narrow),
                preferred_element_type=jnp.float32,
            )
            / sequence_number_overall
        )
        product = (
            product.reshape(block_extent, PRODUCT_FEATURE, block_extent, narrow)
            .transpose(1, 3, 0, 2)
            .astype(jnp.bfloat16)
            .reshape(PRODUCT_FEATURE * narrow, cell_count)
        )
        return jnp.dot(weight_flat, product, preferred_element_type=jnp.float32)

    partials = lax.map(outer_one, chosen)
    summed = lax.psum_scatter(partials, "ch", scatter_dimension=1, tiled=True)
    keep_mask = block_present_flag[0].astype(jnp.float32)
    pairwise_output = (
        pair_field + keep_mask[:, None, None] * (summed + product_result_offset[None, :, None])
    ).astype(jnp.bfloat16)
    return (sequence_result_matrix, pairwise_output)


def solution(mesh):
    return jax.shard_map(
        on_device,
        mesh=mesh,
        in_specs=(
            P(None, "res", None),
            P("res", "ch", None),
            P("res", None),
            P("res", None),
            P("res"),
            P(),
            P(None, None, "ch"),
            P("ch", None),
            P(),
            P("ch"),
            P("ch", None),
            P(),
            P(),
            P(None, "ch"),
            P(None, None, "ch"),
            P("ch"),
        ),
        out_specs=(P(None, "res", None), P("res", "ch", None)),
        check_vma=False,
    )
```

profile of v0, /device:TPU:0, one launch (start us, length us, event | category | flops | bytes accessed | tf_op | source)
XLA Modules:
  0.0 450.4 jit_solution(9530738559762649015)
XLA Ops:
  7.2 7.5 %all-to-all-start = ((bf16[8,64,256]{2,1,0:T(8,128)(2,1)}), bf16[8,64,256]{2,1,0:T(8,128)(2,1)S(1)}, u32[]{:S(2)}, u32[]{:S(2)}) async-start(bf16[8,64,256]{2,1,0:T(8,128)(2,1)} %param.18), calls=%async_computation | async-start | bytes 524288 | tf_op jit(solution)/shard_map/all_to_all | solution.py:69
  14.7 2.4 convert_reduce_fusion
  17.2 1.2 dynamic-slice
  19.1 0.9 dynamic-update-slice
  20.0 11.8 %all-reduce = s32[512]{0:T(512)S(1)} all-reduce(s32[512]{0:T(512)S(1)} %dynamic-update-slice), channel_id=1, replica_groups=mesh['res'=8,'ch'=4] {'res'}, use_global_device_ids=true, to_apply=%add | all-reduce | flops 512 | bytes 4096
  31.9 17.9 %all-gather = s32[8,1,4]{2,1,0:T(1,128)S(1)} all-gather(s32[1,1,4]{2,1,0:T(1,128)} %bitcast.164), channel_id=1, replica_groups=mesh['res'=8,'ch'=4] {'res'}, dimensions={0}, use_global_device_ids=true | all-gather | bytes 144 | tf_op jit(solution)/shard_map/all_gather | solution.py:65
  50.6 1.3 compare_convert_fusion
  51.9 16.8 %all-gather.1 = s32[8,1,4]{2,1,0:T(1,128)S(1)} all-gather(s32[1,1,4]{2,1,0:T(1,128)S(1)} %bitcast.165), channel_id=1, replica_groups=mesh['res'=8,'ch'=4] {'res'}, dimensions={0}, use_global_device_ids=true | all-gather | bytes 144 | tf_op jit(solution)/shard_map/all_gather | solution.py:66
  69.0 0.6 dynamic-slice.1
  70.3 0.9 broadcast_multiply_fusion
  71.2 1.5 convolution_bitcast_fusion.1
  73.0 16.4 %all-reduce.10 = bf16[8,4,4096]{2,1,0:T(4,128)(2,1)S(1)} all-reduce(f32[8,4,4096]{2,1,0:T(4,128)S(1)} %copy.104), channel_id=2, replica_groups=mesh['res'=8,'ch'=4] {'ch'}, use_global_device_ids=true, to_apply=%region_6.0.clone | all-reduce | flops 131072 | bytes 786432
  89.5 31.4 %all_gather.17 = bf16[2,32,4096]{2,0,1:T(2,128)(2,1)S(1)} all-gather(bf16[2,4,4096]{2,0,1:T(2,128)(2,1)S(1)} %copy.105), channel_id=1, replica_groups=mesh['res'=8,'ch'=4] {'res'}, dimensions={1}, use_global_device_ids=true | all-gather | bytes 589824 | tf_op jit(solution)/shard_map/all_gather | solution.py:64
  121.3 2.2 reshape.314
  123.5 1.9 copy.107
  127.3 0.6 gather_fusion.1
  128.1 1.0 reshape.315
  129.1 1.4 gather_fusion
  130.5 0.8 reshape.312
  131.3 2.1 fusion.31
  133.8 0.7 copy-done.3
  135.3 1.0 fusion.33
  136.4 31.8 %all-reduce.7.cloned.1.call-done = f32[512,256]{1,0:T(8,128)} async-done(((f32[512,256]{1,0:T(8,128)}), f32[512,256]{1,0:T(8,128)}) %all-reduce.7.cloned.1.call-update) | async-done | bytes 524304 | tf_op jit(solution)/shard_map/psum | solution.py:142
  168.2 1.1 fusion.22
  170.2 2.2 reduce.8
  172.4 0.8 reshape.378
  173.2 5.6 %all-to-all-start.1 = ((bf16[8,2,8192]{2,1,0:T(2,128)(2,1)}), bf16[8,2,8192]{2,1,0:T(2,128)(2,1)S(1)}, u32[]{:S(2)}, u32[]{:S(2)}) async-start(bf16[8,2,8192]{2,1,0:T(2,128)(2,1)} %reshape.378), calls=%async_computation.1 | async-start | bytes 524288 | tf_op jit(solution)/shard_map/all_to_all | solution.py:148
  179.1 8.0 %all-to-all-done.1 = bf16[8,2,8192]{2,1,0:T(2,128)(2,1)S(1)} async-done(((bf16[8,2,8192]{2,1,0:T(2,128)(2,1)}), bf16[8,2,8192]{2,1,0:T(2,128)(2,1)S(1)}, u32[]{:S(2)}, u32[]{:S(2)}) %all-to-all-start.1) | async-done | bytes 262176 | tf_op jit(solution)/shard_map/all_to_all | solution.py:148
  187.9 1.3 convert_reduce_fusion.2
  189.2 7.4 %multiply_reduce_fusion = f32[512]{0:T(512)S(1)} fusion(f32[512]{0:T(512)S(1)} %broadcast_multiply_fusion.2, bf16[512,1,256]{2,1,0:T(2,128)(2,1)S(1)} %reshape.379), kind=kLoop, calls=%fused_computation.49 | loop fusion | flops 523776 | bytes 266240 | tf_op jit(solution)/shard_map/reduce_sum | solution.py:18
  197.2 33.1 %all_gather.19 = bf16[8,512,8]{2,0,1:T(8,128)(2,1)S(1)} all-gather(bf16[8,64,8]{2,0,1:T(8,128)(2,1)S(1)} %copy.113), channel_id=1, replica_groups=mesh['res'=8,'ch'=4] {'res'}, dimensions={1}, use_global_device_ids=true | all-gather | bytes 73728 | tf_op jit(solution)/shard_map/all_gather | solution.py:172
  230.8 0.7 gather_fusion.3
  231.6 139.8 %while.2 = (s32[]{:T(128)}, f32[4,128,4096]{2,1,0:T(8,128)}, bf16[4,8,64,8]{3,1,2,0:T(8,128)(2,1)S(1)}, bf16[2048,8]{0,1:T(8,128)(2,1)S(1)}, bf16[128,256]{1,0:T(8,128)(2,1)S(1)}, /*index=5*/s32[]{:T(128)}) while((s32[]{:T(128)}, f32[4,128,4096]{2,1,0:T(8,128)}, bf16[4,8,64,8]{3,1,2,0:T(8,128)(2,1)S(1)}, bf16[2048,8]{0,1:T(8,128)(2,1)S(1)}, ...), condition=%wide.region_13.14_spmd, body=%wide.region_12.13_spmd.sunk | while | flops 287309824 | bytes 27418708 | solution.py:203
  231.8 0.8 fusion.55
  232.6 8.1 %convert_element_type.203 = bf16[64,32,64,8]{1,0,3,2:T(8,128)(2,1)} reshape(bf16[2048,512]{0,1:T(8,128)(2,1)S(1)} %fusion.55) | data formatting | bytes 4194304 | tf_op jit(solution)/shard_map/while/body/eval_jaxpr/convert_element_type | solution.py:198
  240.7 14.6 %copy.154 = bf16[32,8,64,64]{3,2,1,0:T(8,128)(2,1)} copy(bf16[32,8,64,64]{0,2,1,3:T(8,128)(2,1)} %bitcast.151) | data formatting | bytes 4194304 | tf_op jit(solution)/shard_map/while/body/eval_jaxpr/convert_element_type | solution.py:198
  255.3 5.7 %reshape.383 = bf16[256,4096]{1,0:T(8,128)(2,1)S(1)} reshape(bf16[32,8,64,64]{3,2,1,0:T(8,128)(2,1)} %copy.154) | data formatting | bytes 4194304 | tf_op jit(solution)/shard_map/while/body/eval_jaxpr/reshape | solution.py:199
  261.0 2.2 convolution_bitcast_fusion.4
  263.1 1.9 copy.155
  265.1 1.5 constant_dynamic-update-slice_fusion.2
  266.8 0.8 fusion.55
  267.6 8.1 %convert_element_type.203 = bf16[64,32,64,8]{1,0,3,2:T(8,128)(2,1)} reshape(bf16[2048,512]{0,1:T(8,128)(2,1)S(1)} %fusion.55) | data formatting | bytes 4194304 | tf_op jit(solution)/shard_map/while/body/eval_jaxpr/convert_element_type | solution.py:198
  275.7 14.6 %copy.154 = bf16[32,8,64,64]{3,2,1,0:T(8,128)(2,1)} copy(bf16[32,8,64,64]{0,2,1,3:T(8,128)(2,1)} %bitcast.151) | data formatting | bytes 4194304 | tf_op jit(solution)/shard_map/while/body/eval_jaxpr/convert_element_type | solution.py:198
  290.3 5.7 %reshape.383 = bf16[256,4096]{1,0:T(8,128)(2,1)S(1)} reshape(bf16[32,8,64,64]{3,2,1,0:T(8,128)(2,1)} %copy.154) | data formatting | bytes 4194304 | tf_op jit(solution)/shard_map/while/body/eval_jaxpr/reshape | solution.py:199
  296.0 2.2 convolution_bitcast_fusion.4
  298.1 1.9 copy.155
  300.1 1.4 constant_dynamic-update-slice_fusion.2
  301.7 0.8 fusion.55
  302.5 8.1 %convert_element_type.203 = bf16[64,32,64,8]{1,0,3,2:T(8,128)(2,1)} reshape(bf16[2048,512]{0,1:T(8,128)(2,1)S(1)} %fusion.55) | data formatting | bytes 4194304 | tf_op jit(solution)/shard_map/while/body/eval_jaxpr/convert_element_type | solution.py:198
  310.6 14.6 %copy.154 = bf16[32,8,64,64]{3,2,1,0:T(8,128)(2,1)} copy(bf16[32,8,64,64]{0,2,1,3:T(8,128)(2,1)} %bitcast.151) | data formatting | bytes 4194304 | tf_op jit(solution)/shard_map/while/body/eval_jaxpr/convert_element_type | solution.py:198
  325.2 5.7 %reshape.383 = bf16[256,4096]{1,0:T(8,128)(2,1)S(1)} reshape(bf16[32,8,64,64]{3,2,1,0:T(8,128)(2,1)} %copy.154) | data formatting | bytes 4194304 | tf_op jit(solution)/shard_map/while/body/eval_jaxpr/reshape | solution.py:199
  330.9 2.2 convolution_bitcast_fusion.4
  333.0 1.9 copy.155
  335.0 1.5 constant_dynamic-update-slice_fusion.2
  336.7 0.8 fusion.55
  337.4 8.1 %convert_element_type.203 = bf16[64,32,64,8]{1,0,3,2:T(8,128)(2,1)} reshape(bf16[2048,512]{0,1:T(8,128)(2,1)S(1)} %fusion.55) | data formatting | bytes 4194304 | tf_op jit(solution)/shard_map/while/body/eval_jaxpr/convert_element_type | solution.py:198
  345.6 14.6 %copy.154 = bf16[32,8,64,64]{3,2,1,0:T(8,128)(2,1)} copy(bf16[32,8,64,64]{0,2,1,3:T(8,128)(2,1)} %bitcast.151) | data formatting | bytes 4194304 | tf_op jit(solution)/shard_map/while/body/eval_jaxpr/convert_element_type | solution.py:198
  360.2 5.7 %reshape.383 = bf16[256,4096]{1,0:T(8,128)(2,1)S(1)} reshape(bf16[32,8,64,64]{3,2,1,0:T(8,128)(2,1)} %copy.154) | data formatting | bytes 4194304 | tf_op jit(solution)/shard_map/while/body/eval_jaxpr/reshape | solution.py:199
  365.8 2.2 convolution_bitcast_fusion.4
  368.0 1.9 copy.155
  369.9 1.5 constant_dynamic-update-slice_fusion.2
  371.5 0.7 copy.126
  372.2 68.8 %reduce-scatter.2.cloned.1.call-done = f32[4,32,4096]{2,1,0:T(8,128)} async-done(((f32[4,128,4096]{2,1,0:T(8,128)}), f32[4,32,4096]{2,1,0:T(8,128)}) %reduce-scatter.2.cloned.1.call-update) | async-done | bytes 2097168 | tf_op jit(solution)/shard_map/reduce_scatter | solution.py:204
  441.0 3.0 fusion.5
  (109 shorter events, 9.3 us)
Async XLA Ops:
  7.2 119.0 %copy-start = (bf16[4,256,64]{1,2,0:T(8,128)(2,1)S(1)}, bf16[4,256,64]{1,2,0:T(8,128)(2,1)}, u32[]{:S(2)}) copy-start(bf16[4,256,64]{1,2,0:T(8,128)(2,1)} %param.24) | copy-start | bytes 393220
  7.2 61.8 %copy-start.17 = (u32[32]{0:T(128)S(1)}, u32[32]{0:T(128)}, u32[]{:S(2)}) copy-start(u32[32]{0:T(128)} %constant.112) | copy-start | bytes 388
  7.2 64.0 %copy-start.1 = (bf16[4,32,4096]{2,1,0:T(8,128)(2,1)S(1)}, bf16[4,32,4096]{2,1,0:T(8,128)(2,1)}, u32[]{:S(2)}) copy-start(bf16[4,32,4096]{2,1,0:T(8,128)(2,1)} %param.19) | copy-start | bytes 3145732
  7.2 44.7 %copy-start.13 = (s32[1,4]{1,0:T(1,128)S(1)}, s32[1,4]{1,0:T(1,128)}, u32[]{:S(2)}) copy-start(s32[1,4]{1,0:T(1,128)} %param.21) | copy-start | bytes 52
  7.2 61.7 %copy-start.15 = (f32[8]{0:T(128)S(1)}, f32[8]{0:T(128)}, u32[]{:S(2)}) copy-start(f32[8]{0:T(128)} %param.26) | copy-start | bytes 100
  7.2 64.0 %copy-start.16 = (f32[32]{0:T(128)S(1)}, f32[32]{0:T(128)}, u32[]{:S(2)}) copy-start(f32[32]{0:T(128)} %param.27) | copy-start | bytes 388
  7.2 64.0 %copy-start.14 = (f32[32,8]{0,1:T(8,128)S(1)}, f32[32,8]{0,1:T(8,128)}, u32[]{:S(2)}) copy-start(f32[32,8]{0,1:T(8,128)} %param.28) | copy-start | bytes 3076
  7.2 118.2 %all-to-all-start = ((bf16[8,64,256]{2,1,0:T(8,128)(2,1)}), bf16[8,64,256]{2,1,0:T(8,128)(2,1)S(1)}, u32[]{:S(2)}, u32[]{:S(2)}) async-start(bf16[8,64,256]{2,1,0:T(8,128)(2,1)} %param.18), calls=%async_computation | async-start | bytes 524288 | tf_op jit(solution)/shard_map/all_to_all | solution.py:69
  14.7 55.5 %all-reduce.9.cloned.1.call-start = ((), (), s32[]{:S(2)}) async-start(), calls=%async_computation.5 | async-start | bytes 262144 | tf_op jit(solution)/shard_map/psum | solution.py:50
  17.1 151.0 %all-reduce.7.cloned.1.call-start = ((), (), s32[]{:S(2)}) async-start(), calls=%async_computation.3 | async-start | bytes 1048576 | tf_op jit(solution)/shard_map/psum | solution.py:142
  123.5 2.5 copy-start.9
  133.4 1.0 copy-start.3
  133.4 1.1 copy-start.4
  134.5 0.8 copy-start.6
  136.3 42.6 %copy-start.5 = (bf16[128,32,8]{0,2,1:T(8,128)(2,1)S(1)}, bf16[128,32,8]{0,2,1:T(8,128)(2,1)}, u32[]{:S(2)}) copy-start(bf16[128,32,8]{0,2,1:T(8,128)(2,1)} %param.32) | copy-start | bytes 196612
  136.3 42.7 %copy-start.12 = (s32[1,4]{1,0:T(1,128)S(1)}, s32[1,4]{1,0:T(1,128)}, u32[]{:S(2)}) copy-start(s32[1,4]{1,0:T(1,128)} %param.20) | copy-start | bytes 52
  172.4 24.2 %copy-start.10 = (f32[256]{0:T(256)S(1)}, f32[256]{0:T(256)}, u32[]{:S(2)}) copy-start(f32[256]{0:T(256)} %param.29) | copy-start | bytes 3076
  173.2 23.6 %copy-start.8 = (bf16[256,8]{0,1:T(8,128)(2,1)S(1)}, bf16[256,8]{0,1:T(8,128)(2,1)}, u32[]{:S(2)}) copy-start(bf16[256,8]{0,1:T(8,128)(2,1)} %param.31) | copy-start | bytes 12292
  173.2 13.9 %all-to-all-start.1 = ((bf16[8,2,8192]{2,1,0:T(2,128)(2,1)}), bf16[8,2,8192]{2,1,0:T(2,128)(2,1)S(1)}, u32[]{:S(2)}, u32[]{:S(2)}) async-start(bf16[8,2,8192]{2,1,0:T(2,128)(2,1)} %reshape.378), calls=%async_computation.1 | async-start | bytes 524288 | tf_op jit(solution)/shard_map/all_to_all | solution.py:148
  178.8 262.1 %reduce-scatter.2.cloned.1.call-start = ((), (), s32[]{:S(2)}) async-start(), calls=%async_computation.4 | async-start | bytes 10485760 | tf_op jit(solution)/shard_map/reduce_scatter | solution.py:204
  187.3 43.0 %copy-start.7 = (bf16[256,32]{0,1:T(8,128)(2,1)S(1)}, bf16[256,32]{0,1:T(8,128)(2,1)}, u32[]{:S(2)}) copy-start(bf16[256,32]{0,1:T(8,128)(2,1)} %param.30) | copy-start | bytes 49156
  371.4 69.5 %copy-start.2 = (bf16[4,32,4096]{2,1,0:T(8,128)(2,1)S(1)}, bf16[4,32,4096]{2,1,0:T(8,128)(2,1)}, u32[]{:S(2)}) copy-start(bf16[4,32,4096]{2,1,0:T(8,128)(2,1)} %param.19) | copy-start | bytes 3145732
  371.4 69.5 %copy-start.11 = (f32[32]{0:T(128)S(1)}, f32[32]{0:T(128)}, u32[]{:S(2)}) copy-start(f32[32]{0:T(128)} %param.33) | copy-start | bytes 388
Sparse Core Ops, SparseCore 0:
  18.5 33.1 all-reduce.8
  136.5 31.6 all-reduce.6
  371.6 69.3 reduce-scatter.1
where the time goes:
time: 452 us; the launch traced here: 450 us
  local copies, waits for them, and re-layouts  146 us (32%)
  blocking collectives  127 us (28%)
  waiting for transfers between devices  109 us (24%)
  other arithmetic  21.8 us (5%)
  matrix products  17.3 us (4%)
  between operations  15.5 us (3%)
  starting transfers between devices  13.2 us (3%)
    convert_element_type x8, local copies, waits for them, and re-layouts, outer_one(): product = product.reshape(block_extent, PRODUCT_FEATURE, block_extent, na...  90.9 us
    reduce_scatter x1, waiting for transfers between devices, on_device(): summed = lax.psum_scatter(partials, 'ch', scatter_dimension=1, tiled=True)  68.8 us
    all_gather x1, blocking collectives, on_device(): shard_piece = lax.all_gather(right_projected, 'res', axis=1, tiled=True)  33.1 us
    psum x1, waiting for transfers between devices, on_device(): head_total = lax.psum(partial_out, 'ch')  31.8 us
    all_gather x1, blocking collectives, on_device(): lax.all_gather(head_bias, 'res', axis=1, tiled=True)  31.4 us
    unnamed x2, blocking collectives  28.2 us
    reshape x4, local copies, waits for them, and re-layouts, outer_one(): product = product.reshape(block_extent, PRODUCT_FEATURE, block_extent, na...  22.7 us
    all_gather x1, blocking collectives, on_device(): lax.all_gather(block_target_entry, 'res', axis=0, tiled=True)  17.9 us
  transfers between devices with their start and end apart: 5, of which 3 were waited for; matrix products, arithmetic and copies ran while one was open for 4% of the time, Pallas kernels for 0%

commit v1 on v0

--- a/solution.py
+++ b/solution.py
@@ -10,6 +10,15 @@
 PRODUCT_FEATURE = 32
 EPS = 1e-05
 MASKED = -1e30
+
+
+def map_point(base_x, which_dim):
+    base_x = jnp.moveaxis(base_x, 0, which_dim)
+    x_new = base_x.shape
+    x_next = base_x.reshape(
+        *x_new[:which_dim], x_new[which_dim] * x_new[which_dim + 1], *x_new[which_dim + 2 :]
+    )
+    return x_next
 
 
 def final_dimension_standardize(values, gain_vector):
@@ -169,7 +178,23 @@
     empty_tiles = jnp.zeros(
         (slot_count, sequence_number_overall, block_extent, narrow), jnp.bfloat16
     )
-    shard_piece = lax.all_gather(right_projected, "res", axis=1, tiled=True)
+    width = lax.axis_size("res")
+    cards = []
+    for hop_no in range(width):
+        cards.append((hop_no, (hop_no + 1) % width))
+    heap = []
+    for kk, q in cards:
+        heap.append((q, kk))
+    p_next, w_next = ([], [])
+    for rr in range(width - 1):
+        if rr % 2 == 0:
+            p_next.append(lax.ppermute(p_next[-1] if p_next else right_projected, "res", cards))
+        else:
+            w_next.append(lax.ppermute(w_next[-1] if w_next else right_projected, "res", heap))
+    piece_now = jnp.stack([*p_next[::-1], right_projected, *w_next], axis=0)
+    current_arr = lax.axis_index("res") - len(p_next)
+    piece_now = piece_now[(jnp.arange(width) - current_arr) % width]
+    shard_piece = map_point(piece_now, 1)
     piece_rows = shard_piece.shape[1]
     offset = own_columns * block_extent
     inside = (offset >= 0) & (offset < piece_rows)

time: 452 us -> 448 us (level)
  blocking collectives: 127 us -> 94.3 us
  starting transfers between devices: 13.2 us -> 28.9 us
  waiting for transfers between devices: 109 us -> 122 us
    all_gather x1 -> x0, blocking collectives: 33.1 us -> none  [on_device(): shard_piece = lax.all_gather(right_projected, 'res', axis=1, tiled=True)]
    ppermute x0 -> x7, starting transfers between devices: none -> 15.7 us  [the longest x3 14.3 us: on_device(): lax.ppermute(w_next[-1] if w_next else right_projected, 'res', heap)]
    ppermute x0 -> x7, waiting for transfers between devices: none -> 9.62 us  [the longest x4 9.3 us: on_device(): lax.ppermute(p_next[-1] if p_next else right_projected, 'res', cards)]
  transfers between devices with their start and end apart: 5 -> 12, of which waited for: 3 -> 8; matrix products, arithmetic and copies ran while one was open for 4% -> 4% of each run, Pallas kernels for 0% -> 0%
where the time goes in v1:
time: 448 us; the launch traced here: 447 us
  local copies, waits for them, and re-layouts  148 us (33%)
  waiting for transfers between devices  122 us (27%)
  blocking collectives  94.3 us (21%)
  starting transfers between devices  28.9 us (6%)
  other arithmetic  21.8 us (5%)
  matrix products  17.2 us (4%)
  between operations  15.5 us (3%)
    convert_element_type x8, local copies, waits for them, and re-layouts, outer_one(): product = product.reshape(block_extent, PRODUCT_FEATURE, block_extent, na...  90.9 us
    reduce_scatter x1, waiting for transfers between devices, on_device(): summed = lax.psum_scatter(partials, 'ch', scatter_dimension=1, tiled=True)  71.9 us
    psum x1, waiting for transfers between devices, on_device(): head_total = lax.psum(partial_out, 'ch')  31.8 us
    all_gather x1, blocking collectives, on_device(): lax.all_gather(head_bias, 'res', axis=1, tiled=True)  31.4 us
    unnamed x2, blocking collectives  28.2 us
    reshape x4, local copies, waits for them, and re-layouts, outer_one(): product = product.reshape(block_extent, PRODUCT_FEATURE, block_extent, na...  22.7 us
    all_gather x1, blocking collectives, on_device(): lax.all_gather(block_target_entry, 'res', axis=0, tiled=True)  17.9 us
    all_gather x1, blocking collectives, on_device(): lax.all_gather(block_present_flag, 'res', axis=0, tiled=True)  16.8 us
  transfers between devices with their start and end apart: 12, of which 8 were waited for; matrix products, arithmetic and copies ran while one was open for 4% of the time, Pallas kernels for 0%

profile of v1, /device:TPU:0, one launch (start us, length us, event | category | flops | bytes accessed | tf_op | source)
XLA Modules:
  0.0 446.9 jit_solution(1716009650096445688)
XLA Ops:
  7.2 7.5 %all-to-all-start = ((bf16[8,64,256]{2,1,0:T(8,128)(2,1)}), bf16[8,64,256]{2,1,0:T(8,128)(2,1)S(1)}, u32[]{:S(2)}, u32[]{:S(2)}) async-start(bf16[8,64,256]{2,1,0:T(8,128)(2,1)} %param.18), calls=%async_computation | async-start | bytes 524288 | tf_op jit(solution)/shard_map/all_to_all | solution.py:78
  14.7 2.4 convert_reduce_fusion
  17.2 1.2 dynamic-slice
  19.1 0.9 dynamic-update-slice
  20.0 11.8 %all-reduce = s32[512]{0:T(512)S(1)} all-reduce(s32[512]{0:T(512)S(1)} %dynamic-update-slice), channel_id=1, replica_groups=mesh['res'=8,'ch'=4] {'res'}, use_global_device_ids=true, to_apply=%add | all-reduce | flops 512 | bytes 4096
  31.9 17.9 %all-gather = s32[8,1,4]{2,1,0:T(1,128)S(1)} all-gather(s32[1,1,4]{2,1,0:T(1,128)} %bitcast.186), channel_id=1, replica_groups=mesh['res'=8,'ch'=4] {'res'}, dimensions={0}, use_global_device_ids=true | all-gather | bytes 144 | tf_op jit(solution)/shard_map/all_gather | solution.py:74
  50.6 1.3 compare_convert_fusion
  51.9 16.8 %all-gather.1 = s32[8,1,4]{2,1,0:T(1,128)S(1)} all-gather(s32[1,1,4]{2,1,0:T(1,128)S(1)} %bitcast.187), channel_id=1, replica_groups=mesh['res'=8,'ch'=4] {'res'}, dimensions={0}, use_global_device_ids=true | all-gather | bytes 144 | tf_op jit(solution)/shard_map/all_gather | solution.py:75
  70.3 0.9 broadcast_multiply_fusion
  71.2 1.5 convolution_bitcast_fusion.1
  73.0 16.4 %all-reduce.10 = bf16[8,4,4096]{2,1,0:T(4,128)(2,1)S(1)} all-reduce(f32[8,4,4096]{2,1,0:T(4,128)S(1)} %copy.104), channel_id=2, replica_groups=mesh['res'=8,'ch'=4] {'ch'}, use_global_device_ids=true, to_apply=%region_6.0.clone | all-reduce | flops 131072 | bytes 786432
  89.5 31.4 %all_gather.14 = bf16[2,32,4096]{2,0,1:T(2,128)(2,1)S(1)} all-gather(bf16[2,4,4096]{2,0,1:T(2,128)(2,1)S(1)} %copy.105), channel_id=1, replica_groups=mesh['res'=8,'ch'=4] {'res'}, dimensions={1}, use_global_device_ids=true | all-gather | bytes 589824 | tf_op jit(solution)/shard_map/all_gather | solution.py:73
  121.3 2.2 reshape.367
  123.4 1.9 copy.107
  128.1 1.0 reshape.368
  129.1 1.4 gather_fusion
  130.5 0.8 reshape.365
  131.3 2.1 fusion.33
  135.3 1.0 fusion.35
  136.3 31.8 %all-reduce.7.cloned.1.call-done = f32[512,256]{1,0:T(8,128)} async-done(((f32[512,256]{1,0:T(8,128)}), f32[512,256]{1,0:T(8,128)}) %all-reduce.7.cloned.1.call-update) | async-done | bytes 524304 | tf_op jit(solution)/shard_map/psum | solution.py:151
  168.1 1.1 fusion.22
  170.2 2.2 reduce.8
  172.4 0.8 reshape.439
  173.2 5.6 %all-to-all-start.1 = ((bf16[8,2,8192]{2,1,0:T(2,128)(2,1)}), bf16[8,2,8192]{2,1,0:T(2,128)(2,1)S(1)}, u32[]{:S(2)}, u32[]{:S(2)}) async-start(bf16[8,2,8192]{2,1,0:T(2,128)(2,1)} %reshape.439), calls=%async_computation.1 | async-start | bytes 524288 | tf_op jit(solution)/shard_map/all_to_all | solution.py:157
  178.9 8.1 %all-to-all-done.1 = bf16[8,2,8192]{2,1,0:T(2,128)(2,1)S(1)} async-done(((bf16[8,2,8192]{2,1,0:T(2,128)(2,1)}), bf16[8,2,8192]{2,1,0:T(2,128)(2,1)S(1)}, u32[]{:S(2)}, u32[]{:S(2)}) %all-to-all-start.1) | async-done | bytes 262176 | tf_op jit(solution)/shard_map/all_to_all | solution.py:157
  187.9 1.3 convert_reduce_fusion.2
  189.1 7.4 %multiply_reduce_fusion = f32[512]{0:T(512)S(1)} fusion(f32[512]{0:T(512)S(1)} %broadcast_multiply_fusion.2, bf16[512,1,256]{2,1,0:T(2,128)(2,1)S(1)} %reshape.440), kind=kLoop, calls=%fused_computation.50 | loop fusion | flops 523776 | bytes 266240 | tf_op jit(solution)/shard_map/reduce_sum | solution.py:27
  197.0 1.4 collective-permute-start
  198.4 5.1 %collective-permute-done = bf16[8,64,8]{1,0,2:T(8,128)(2,1)S(1)} collective-permute-done((bf16[8,64,8]{1,0,2:T(8,128)(2,1)S(1)}, bf16[8,64,8]{1,0,2:T(8,128)(2,1)S(1)}, u32[]{:S(2)}, u32[]{:S(2)}) %collective-permute-start) | collective-permute-done | bytes 8224 | tf_op jit(solution)/shard_map/ppermute | solution.py:191
  203.5 4.8 %collective-permute-start.4 = (bf16[8,64,8]{1,0,2:T(8,128)(2,1)S(1)}, bf16[8,64,8]{1,0,2:T(8,128)(2,1)S(1)}, u32[]{:S(2)}, u32[]{:S(2)}) collective-permute-start(bf16[8,64,8]{1,0,2:T(8,128)(2,1)S(1)} %reshape.358), channel_id=1, source_target_pairs={{4,0},{8,4},{12,8},{16,12},{20,16},{24,20},{28,24},{0,28},{5,1},{9... | collective-permute-start | bytes 24584 | tf_op jit(solution)/shard_map/ppermute | solution.py:193
  208.3 1.6 collective-permute-done.1
  210.1 4.8 %collective-permute-start.5 = (bf16[8,64,8]{1,0,2:T(8,128)(2,1)S(1)}, bf16[8,64,8]{1,0,2:T(8,128)(2,1)S(1)}, u32[]{:S(2)}, u32[]{:S(2)}) collective-permute-start(bf16[8,64,8]{1,0,2:T(8,128)(2,1)S(1)} %collective-permute-done.4), channel_id=1, source_target_pairs={{4,0},{8,4},{12,8},{16,12},{20,16},{24,20},{28,24},{0,28},{5,1},{9... | collective-permute-start | bytes 24584 | tf_op jit(solution)/shard_map/ppermute | solution.py:193
  214.8 1.5 collective-permute-done.2
  217.0 4.8 %collective-permute-start.6 = (bf16[8,64,8]{1,0,2:T(8,128)(2,1)S(1)}, bf16[8,64,8]{1,0,2:T(8,128)(2,1)S(1)}, u32[]{:S(2)}, u32[]{:S(2)}) collective-permute-start(bf16[8,64,8]{1,0,2:T(8,128)(2,1)S(1)} %collective-permute-done.5), channel_id=1, source_target_pairs={{4,0},{8,4},{12,8},{16,12},{20,16},{24,20},{28,24},{0,28},{5,1},{9... | collective-permute-start | bytes 24584 | tf_op jit(solution)/shard_map/ppermute | solution.py:193
  221.7 1.1 collective-permute-done.3
  225.1 139.6 %while.2 = (s32[]{:T(128)}, f32[4,128,4096]{2,1,0:T(8,128)}, bf16[4,8,64,8]{3,1,2,0:T(8,128)(2,1)S(1)}, bf16[2048,8]{0,1:T(8,128)(2,1)S(1)}, bf16[128,256]{1,0:T(8,128)(2,1)S(1)}, /*index=5*/s32[]{:T(128)}) while((s32[]{:T(128)}, f32[4,128,4096]{2,1,0:T(8,128)}, bf16[4,8,64,8]{3,1,2,0:T(8,128)(2,1)S(1)}, bf16[2048,8]{0,1:T(8,128)(2,1)S(1)}, ...), condition=%wide.region_13.14_spmd, body=%wide.region_12.13_spmd.sunk | while | flops 287309824 | bytes 27418708 | solution.py:228
  226.1 8.1 %convert_element_type.203 = bf16[64,32,64,8]{1,0,3,2:T(8,128)(2,1)} reshape(bf16[2048,512]{0,1:T(8,128)(2,1)S(1)} %fusion.57) | data formatting | bytes 4194304 | tf_op jit(solution)/shard_map/while/body/eval_jaxpr/convert_element_type | solution.py:223
  234.2 14.6 %copy.154 = bf16[32,8,64,64]{3,2,1,0:T(8,128)(2,1)} copy(bf16[32,8,64,64]{0,2,1,3:T(8,128)(2,1)} %bitcast.171) | data formatting | bytes 4194304 | tf_op jit(solution)/shard_map/while/body/eval_jaxpr/convert_element_type | solution.py:223
  248.9 5.7 %reshape.444 = bf16[256,4096]{1,0:T(8,128)(2,1)S(1)} reshape(bf16[32,8,64,64]{3,2,1,0:T(8,128)(2,1)} %copy.154) | data formatting | bytes 4194304 | tf_op jit(solution)/shard_map/while/body/eval_jaxpr/reshape | solution.py:224
  254.5 2.1 convolution_bitcast_fusion.4
  256.6 1.9 copy.155
  258.6 1.5 constant_dynamic-update-slice_fusion.10
  261.0 8.1 %convert_element_type.203 = bf16[64,32,64,8]{1,0,3,2:T(8,128)(2,1)} reshape(bf16[2048,512]{0,1:T(8,128)(2,1)S(1)} %fusion.57) | data formatting | bytes 4194304 | tf_op jit(solution)/shard_map/while/body/eval_jaxpr/convert_element_type | solution.py:223
  269.1 14.6 %copy.154 = bf16[32,8,64,64]{3,2,1,0:T(8,128)(2,1)} copy(bf16[32,8,64,64]{0,2,1,3:T(8,128)(2,1)} %bitcast.171) | data formatting | bytes 4194304 | tf_op jit(solution)/shard_map/while/body/eval_jaxpr/convert_element_type | solution.py:223
  283.8 5.7 %reshape.444 = bf16[256,4096]{1,0:T(8,128)(2,1)S(1)} reshape(bf16[32,8,64,64]{3,2,1,0:T(8,128)(2,1)} %copy.154) | data formatting | bytes 4194304 | tf_op jit(solution)/shard_map/while/body/eval_jaxpr/reshape | solution.py:224
  289.4 2.1 convolution_bitcast_fusion.4
  291.5 1.9 copy.155
  293.5 1.5 constant_dynamic-update-slice_fusion.10
  295.2 0.8 fusion.57
  295.9 8.1 %convert_element_type.203 = bf16[64,32,64,8]{1,0,3,2:T(8,128)(2,1)} reshape(bf16[2048,512]{0,1:T(8,128)(2,1)S(1)} %fusion.57) | data formatting | bytes 4194304 | tf_op jit(solution)/shard_map/while/body/eval_jaxpr/convert_element_type | solution.py:223
  304.0 14.6 %copy.154 = bf16[32,8,64,64]{3,2,1,0:T(8,128)(2,1)} copy(bf16[32,8,64,64]{0,2,1,3:T(8,128)(2,1)} %bitcast.171) | data formatting | bytes 4194304 | tf_op jit(solution)/shard_map/while/body/eval_jaxpr/convert_element_type | solution.py:223
  318.6 5.7 %reshape.444 = bf16[256,4096]{1,0:T(8,128)(2,1)S(1)} reshape(bf16[32,8,64,64]{3,2,1,0:T(8,128)(2,1)} %copy.154) | data formatting | bytes 4194304 | tf_op jit(solution)/shard_map/while/body/eval_jaxpr/reshape | solution.py:224
  324.3 2.1 convolution_bitcast_fusion.4
  326.4 1.9 copy.155
  328.3 1.5 constant_dynamic-update-slice_fusion.10
  330.0 0.8 fusion.57
  330.8 8.1 %convert_element_type.203 = bf16[64,32,64,8]{1,0,3,2:T(8,128)(2,1)} reshape(bf16[2048,512]{0,1:T(8,128)(2,1)S(1)} %fusion.57) | data formatting | bytes 4194304 | tf_op jit(solution)/shard_map/while/body/eval_jaxpr/convert_element_type | solution.py:223
  338.9 14.6 %copy.154 = bf16[32,8,64,64]{3,2,1,0:T(8,128)(2,1)} copy(bf16[32,8,64,64]{0,2,1,3:T(8,128)(2,1)} %bitcast.171) | data formatting | bytes 4194304 | tf_op jit(solution)/shard_map/while/body/eval_jaxpr/convert_element_type | solution.py:223
  353.5 5.7 %reshape.444 = bf16[256,4096]{1,0:T(8,128)(2,1)S(1)} reshape(bf16[32,8,64,64]{3,2,1,0:T(8,128)(2,1)} %copy.154) | data formatting | bytes 4194304 | tf_op jit(solution)/shard_map/while/body/eval_jaxpr/reshape | solution.py:224
  359.2 2.1 convolution_bitcast_fusion.4
  361.3 1.9 copy.155
  363.2 1.5 constant_dynamic-update-slice_fusion.10
  365.5 71.9 %reduce-scatter.2.cloned.1.call-done = f32[4,32,4096]{2,1,0:T(8,128)} async-done(((f32[4,128,4096]{2,1,0:T(8,128)}), f32[4,32,4096]{2,1,0:T(8,128)}) %reduce-scatter.2.cloned.1.call-update) | async-done | bytes 2097168 | tf_op jit(solution)/shard_map/reduce_scatter | solution.py:229
  437.4 3.0 fusion.5
  (134 shorter events, 15.7 us)
Async XLA Ops:
  7.2 119.0 %copy-start = (bf16[4,256,64]{1,2,0:T(8,128)(2,1)S(1)}, bf16[4,256,64]{1,2,0:T(8,128)(2,1)}, u32[]{:S(2)}) copy-start(bf16[4,256,64]{1,2,0:T(8,128)(2,1)} %param.24) | copy-start | bytes 393220
  7.2 61.8 %copy-start.17 = (u32[32]{0:T(128)S(1)}, u32[32]{0:T(128)}, u32[]{:S(2)}) copy-start(u32[32]{0:T(128)} %constant.134) | copy-start | bytes 388
  7.2 64.0 %copy-start.1 = (bf16[4,32,4096]{2,1,0:T(8,128)(2,1)S(1)}, bf16[4,32,4096]{2,1,0:T(8,128)(2,1)}, u32[]{:S(2)}) copy-start(bf16[4,32,4096]{2,1,0:T(8,128)(2,1)} %param.19) | copy-start | bytes 3145732
  7.2 44.7 %copy-start.13 = (s32[1,4]{1,0:T(1,128)S(1)}, s32[1,4]{1,0:T(1,128)}, u32[]{:S(2)}) copy-start(s32[1,4]{1,0:T(1,128)} %param.21) | copy-start | bytes 52
  7.2 61.7 %copy-start.15 = (f32[8]{0:T(128)S(1)}, f32[8]{0:T(128)}, u32[]{:S(2)}) copy-start(f32[8]{0:T(128)} %param.26) | copy-start | bytes 100
  7.2 64.0 %copy-start.16 = (f32[32]{0:T(128)S(1)}, f32[32]{0:T(128)}, u32[]{:S(2)}) copy-start(f32[32]{0:T(128)} %param.27) | copy-start | bytes 388
  7.2 64.0 %copy-start.14 = (f32[32,8]{0,1:T(8,128)S(1)}, f32[32,8]{0,1:T(8,128)}, u32[]{:S(2)}) copy-start(f32[32,8]{0,1:T(8,128)} %param.28) | copy-start | bytes 3076
  7.2 118.1 %all-to-all-start = ((bf16[8,64,256]{2,1,0:T(8,128)(2,1)}), bf16[8,64,256]{2,1,0:T(8,128)(2,1)S(1)}, u32[]{:S(2)}, u32[]{:S(2)}) async-start(bf16[8,64,256]{2,1,0:T(8,128)(2,1)} %param.18), calls=%async_computation | async-start | bytes 524288 | tf_op jit(solution)/shard_map/all_to_all | solution.py:78
  14.7 55.5 %all-reduce.9.cloned.1.call-start = ((), (), s32[]{:S(2)}) async-start(), calls=%async_computation.5 | async-start | bytes 262144 | tf_op jit(solution)/shard_map/psum | solution.py:59
  17.1 151.0 %all-reduce.7.cloned.1.call-start = ((), (), s32[]{:S(2)}) async-start(), calls=%async_computation.3 | async-start | bytes 1048576 | tf_op jit(solution)/shard_map/psum | solution.py:151
  123.4 2.5 copy-start.9
  133.4 1.0 copy-start.3
  133.4 1.1 copy-start.4
  134.5 0.8 copy-start.6
  136.3 42.6 %copy-start.12 = (s32[1,4]{1,0:T(1,128)S(1)}, s32[1,4]{1,0:T(1,128)}, u32[]{:S(2)}) copy-start(s32[1,4]{1,0:T(1,128)} %param.20) | copy-start | bytes 52
  172.4 24.2 %copy-start.10 = (f32[256]{0:T(256)S(1)}, f32[256]{0:T(256)}, u32[]{:S(2)}) copy-start(f32[256]{0:T(256)} %param.29) | copy-start | bytes 3076
  173.2 23.6 %copy-start.8 = (bf16[256,8]{0,1:T(8,128)(2,1)S(1)}, bf16[256,8]{0,1:T(8,128)(2,1)}, u32[]{:S(2)}) copy-start(bf16[256,8]{0,1:T(8,128)(2,1)} %param.31) | copy-start | bytes 12292
  173.2 13.9 %all-to-all-start.1 = ((bf16[8,2,8192]{2,1,0:T(2,128)(2,1)}), bf16[8,2,8192]{2,1,0:T(2,128)(2,1)S(1)}, u32[]{:S(2)}, u32[]{:S(2)}) async-start(bf16[8,2,8192]{2,1,0:T(2,128)(2,1)} %reshape.439), calls=%async_computation.1 | async-start | bytes 524288 | tf_op jit(solution)/shard_map/all_to_all | solution.py:157
  178.8 31.1 %copy-start.5 = (bf16[128,32,8]{0,2,1:T(8,128)(2,1)S(1)}, bf16[128,32,8]{0,2,1:T(8,128)(2,1)}, u32[]{:S(2)}) copy-start(bf16[128,32,8]{0,2,1:T(8,128)(2,1)} %param.32) | copy-start | bytes 196612
  178.8 37.5 %copy-start.7 = (bf16[256,32]{0,1:T(8,128)(2,1)S(1)}, bf16[256,32]{0,1:T(8,128)(2,1)}, u32[]{:S(2)}) copy-start(bf16[256,32]{0,1:T(8,128)(2,1)} %param.30) | copy-start | bytes 49156
  178.8 258.6 %reduce-scatter.2.cloned.1.call-start = ((), (), s32[]{:S(2)}) async-start(), calls=%async_computation.4 | async-start | bytes 10485760 | tf_op jit(solution)/shard_map/reduce_scatter | solution.py:229
  197.0 6.4 %collective-permute-start = (bf16[8,64,8]{1,0,2:T(8,128)(2,1)S(1)}, bf16[8,64,8]{1,0,2:T(8,128)(2,1)S(1)}, u32[]{:S(2)}, u32[]{:S(2)}) collective-permute-start(bf16[8,64,8]{1,0,2:T(8,128)(2,1)S(1)} %reshape.358), channel_id=1, source_target_pairs={{0,4},{4,8},{8,12},{12,16},{16,20},{20,24},{24,28},{28,0},{1,5},{5... | collective-permute-start | bytes 24584 | tf_op jit(solution)/shard_map/ppermute | solution.py:191
  203.5 6.4 %collective-permute-start.1 = (bf16[8,64,8]{1,0,2:T(8,128)(2,1)S(1)}, bf16[8,64,8]{1,0,2:T(8,128)(2,1)S(1)}, u32[]{:S(2)}, u32[]{:S(2)}) collective-permute-start(bf16[8,64,8]{1,0,2:T(8,128)(2,1)S(1)} %collective-permute-done), channel_id=1, source_target_pairs={{0,4},{4,8},{8,12},{12,16},{16,20},{20,24},{24,28},{28,0},{1,5},{5... | collective-permute-start | bytes 24584 | tf_op jit(solution)/shard_map/ppermute | solution.py:191
  203.5 6.6 %collective-permute-start.4 = (bf16[8,64,8]{1,0,2:T(8,128)(2,1)S(1)}, bf16[8,64,8]{1,0,2:T(8,128)(2,1)S(1)}, u32[]{:S(2)}, u32[]{:S(2)}) collective-permute-start(bf16[8,64,8]{1,0,2:T(8,128)(2,1)S(1)} %reshape.358), channel_id=1, source_target_pairs={{4,0},{8,4},{12,8},{16,12},{20,16},{24,20},{28,24},{0,28},{5,1},{9... | collective-permute-start | bytes 24584 | tf_op jit(solution)/shard_map/ppermute | solution.py:193
  209.9 6.4 %collective-permute-start.2 = (bf16[8,64,8]{1,0,2:T(8,128)(2,1)S(1)}, bf16[8,64,8]{1,0,2:T(8,128)(2,1)S(1)}, u32[]{:S(2)}, u32[]{:S(2)}) collective-permute-start(bf16[8,64,8]{1,0,2:T(8,128)(2,1)S(1)} %collective-permute-done.1), channel_id=1, source_target_pairs={{0,4},{4,8},{8,12},{12,16},{16,20},{20,24},{24,28},{28,0},{1,5},{5... | collective-permute-start | bytes 24584 | tf_op jit(solution)/shard_map/ppermute | solution.py:191
  210.1 6.9 %collective-permute-start.5 = (bf16[8,64,8]{1,0,2:T(8,128)(2,1)S(1)}, bf16[8,64,8]{1,0,2:T(8,128)(2,1)S(1)}, u32[]{:S(2)}, u32[]{:S(2)}) collective-permute-start(bf16[8,64,8]{1,0,2:T(8,128)(2,1)S(1)} %collective-permute-done.4), channel_id=1, source_target_pairs={{4,0},{8,4},{12,8},{16,12},{20,16},{24,20},{28,24},{0,28},{5,1},{9... | collective-permute-start | bytes 24584 | tf_op jit(solution)/shard_map/ppermute | solution.py:193
  216.4 6.4 %collective-permute-start.3 = (bf16[8,64,8]{1,0,2:T(8,128)(2,1)S(1)}, bf16[8,64,8]{1,0,2:T(8,128)(2,1)S(1)}, u32[]{:S(2)}, u32[]{:S(2)}) collective-permute-start(bf16[8,64,8]{1,0,2:T(8,128)(2,1)S(1)} %collective-permute-done.2), channel_id=1, source_target_pairs={{0,4},{4,8},{8,12},{12,16},{16,20},{20,24},{24,28},{28,0},{1,5},{5... | collective-permute-start | bytes 24584 | tf_op jit(solution)/shard_map/ppermute | solution.py:191
  217.0 6.2 %collective-permute-start.6 = (bf16[8,64,8]{1,0,2:T(8,128)(2,1)S(1)}, bf16[8,64,8]{1,0,2:T(8,128)(2,1)S(1)}, u32[]{:S(2)}, u32[]{:S(2)}) collective-permute-start(bf16[8,64,8]{1,0,2:T(8,128)(2,1)S(1)} %collective-permute-done.5), channel_id=1, source_target_pairs={{4,0},{8,4},{12,8},{16,12},{20,16},{24,20},{28,24},{0,28},{5,1},{9... | collective-permute-start | bytes 24584 | tf_op jit(solution)/shard_map/ppermute | solution.py:193
  364.7 72.7 %copy-start.2 = (bf16[4,32,4096]{2,1,0:T(8,128)(2,1)S(1)}, bf16[4,32,4096]{2,1,0:T(8,128)(2,1)}, u32[]{:S(2)}) copy-start(bf16[4,32,4096]{2,1,0:T(8,128)(2,1)} %param.19) | copy-start | bytes 3145732
  364.7 72.7 %copy-start.11 = (f32[32]{0:T(128)S(1)}, f32[32]{0:T(128)}, u32[]{:S(2)}) copy-start(f32[32]{0:T(128)} %param.33) | copy-start | bytes 388
Sparse Core Ops, SparseCore 0:
  18.5 33.1 all-reduce.8
  136.5 31.6 all-reduce.6
  364.9 72.5 reduce-scatter.1
